TPU v7x, 32 devices: a whole 2x2x4 slice. The times are simulated.
32 devices in a mesh: groups: 2 (over y), ctx: 4 (over z), head: 2 (over x), tp: 2 (over core).
Axes of the slice: x: 2, y: 2, z: 4, core: 2. Of those that a mesh axis runs over, the one named last changes fastest.
Arguments:
- queries: bfloat16 [32, 2048, 128], P(('head', 'tp'), ('groups', 'ctx')), parts along dimension 1, may hold values from -80 to 80
- stretch_keys: bfloat16 [8, 2048, 128], P(('head', 'tp'), ('groups', 'ctx')), parts along dimension 1, may hold values from -120 to 120
- stretch_values: bfloat16 [8, 2048, 128], P(('head', 'tp'), ('groups', 'ctx')), parts along dimension 1, may hold values from -6 to 6
- cache_keys: bfloat16 [8, 32768, 128], P(('head', 'tp'), ('groups', 'ctx')), parts along dimension 1, may hold values from -6 to 6
- cache_values: bfloat16 [8, 32768, 128], P(('head', 'tp'), ('groups', 'ctx')), parts along dimension 1, may hold values from -6 to 6
- block_picks: int32 [4, 8, 16], P('groups'), parts along dimension 0, may hold values from 0 to 31, as said below
- block_table: int32 [64], P('groups'), parts along dimension 0, may hold values from 0 to 31, as said below
Outputs:
- attended: bfloat16 [32, 2048, 128], P(('head', 'tp'), ('groups', 'ctx')), parts along dimension 1
There are 2 independent parts, one for each index of `groups`. A program takes and returns all parts, laid end to end along the dimension named above; each array names one. Nothing has to cross between parts.
Inputs may be any that keep to these rules, and one draw needn't show every extreme that they name: `block_picks`: for each query block and KV head the 16 picks are different logical blocks; exactly 4 of them have slots on each of 4 different indices of ctx, slot s lying on index s // 8. `block_table`: A permutation of the 32 physical slots.
All inputs are finite; a program needn't handle non-finite values.
Results may differ from a plain program's by a relative error of at most 0.0032.
Values may be sent and summed in bfloat16 or wider, within the bound.
No kernel may reach another device: no remote copies, remote signals or barrier semaphores. Data moves between devices by JAX's collectives and lax.ppermute only.
A program may use at most 64 MiB of HBM per device.

v0:
```python
import jax
import jax.numpy as jnp
import numpy as np
from jax import lax
from jax.sharding import PartitionSpec as P

BLOCK = 512
TOPK = 16


def shifted(value, axis, by):
    count = lax.axis_size(axis)
    pairs = [(i, i + by) for i in range(count) if 0 <= i + by < count]
    return lax.ppermute(value, axis, pairs)


def as_sent(value):

    def short(part):
        return part.astype(jnp.bfloat16) if part.dtype == jnp.float32 else part

    return jax.tree.map(short, value)


def partner(value, axis, bit):
    mask = 2**bit
    pairs = [(source, source ^ mask) for source in range(lax.axis_size(axis))]
    return lax.ppermute(value, axis, pairs)


def lookup(lookup_table, indices):
    entries = jnp.arange(lookup_table.shape[0], dtype=jnp.int32)
    return jnp.sum(jnp.where(indices[..., None] == entries, lookup_table, 0), axis=-1)


def owner_rank(owners):
    ordinal = jnp.arange(owners.shape[-1], dtype=jnp.int32)
    before = (owners[..., :, None] == owners[..., None, :]) & (ordinal[None, :] < ordinal[:, None])
    return jnp.sum(before, axis=-1)


def pick_rows(source, indices):
    return source[indices]


def take_blocks(blocks, indices):
    return jax.vmap(pick_rows)(blocks, indices)


def attend(query_rows, all_keys, all_values, allowed_mask):
    tile_relevance = jnp.einsum(
        "rd,kd->rk", query_rows, all_keys, preferred_element_type=jnp.float32
    )
    tile_relevance = tile_relevance * query_rows.shape[-1] ** (-0.5)
    tile_relevance = jnp.where(allowed_mask, tile_relevance, -jnp.inf)
    row_max = jnp.max(tile_relevance, axis=-1, keepdims=True)
    weights = jnp.exp(tile_relevance - row_max)
    weight_sum = jnp.sum(weights, axis=-1, keepdims=True)
    mixed = jnp.einsum(
        "rk,kd->rd", weights.astype(jnp.bfloat16), all_values, preferred_element_type=jnp.float32
    )
    return (mixed / weight_sum).astype(jnp.bfloat16)


def shards(
    queries, stretch_keys, stretch_values, cache_keys, cache_values, block_picks, block_table
):
    kv_dev, tok_dev, head_dim = stretch_keys.shape
    q_per_kv = queries.shape[0] // kv_dev
    blocks_dev = cache_keys.shape[1] // BLOCK
    ctx_size = lax.axis_size("ctx")
    ctx_index = lax.axis_index("ctx")
    per_peer = max(1, TOPK // ctx_size)
    parity = ctx_index % 2
    head_ids = lax.axis_index(("head", "tp")) * kv_dev + jnp.arange(kv_dev, dtype=jnp.int32)
    selector = head_ids[:, None] == jnp.arange(block_picks.shape[1], dtype=jnp.int32)[None, :]
    my_picks = jnp.sum(jnp.where(selector[None, :, :, None], block_picks[:, None, :, :], 0), axis=2)
    physical = lookup(block_table, my_picks)
    owners = physical // blocks_dev
    in_owner = physical % blocks_dev
    peer_rank = owner_rank(owners)
    targets = np.arange(ctx_size) * tok_dev // BLOCK
    target_owner = owners[targets]
    target_rank = peer_rank[targets]
    target_local = in_owner[targets]
    slot_ids = jnp.arange(per_peer, dtype=jnp.int32)
    matched = (target_owner[:, :, None, :] == ctx_index) & (
        target_rank[:, :, None, :] == slot_ids[None, None, :, None]
    )
    chosen = jnp.sum(jnp.where(matched, target_local[:, :, None, :], 0), axis=-1)
    usable = jnp.any(matched, axis=-1)
    chosen = jnp.transpose(chosen, (1, 0, 2)).reshape(kv_dev, ctx_size * per_peer)
    usable = jnp.transpose(usable, (1, 0, 2)).reshape(kv_dev, ctx_size * per_peer)
    my_block = ctx_index * tok_dev // BLOCK
    my_owner = lax.dynamic_index_in_dim(owners, my_block, 0, keepdims=False)
    my_rank = lax.dynamic_index_in_dim(peer_rank, my_block, 0, keepdims=False)
    my_slot = my_owner * per_peer + my_rank
    prev_keys, prev_values = shifted((stretch_keys, stretch_values), "ctx", 1)
    half_rows = BLOCK // 2
    key_halves = cache_keys.reshape(kv_dev, blocks_dev * 2, half_rows, head_dim)
    value_halves = cache_values.reshape(kv_dev, blocks_dev * 2, half_rows, head_dim)
    row_side = jnp.asarray(np.repeat(np.arange(ctx_size) % 2, per_peer), jnp.int32)
    half_index = chosen * 2 + row_side[None, :]
    sent_keys = jnp.where(usable[:, :, None, None], take_blocks(key_halves, half_index), 0).astype(
        jnp.bfloat16
    )
    sent_values = jnp.where(
        usable[:, :, None, None], take_blocks(value_halves, half_index), 0
    ).astype(jnp.bfloat16)
    got_keys, got_values = (
        lax.all_to_all(sent_keys, "ctx", split_axis=1, concat_axis=1, tiled=True),
        lax.all_to_all(sent_values, "ctx", split_axis=1, concat_axis=1, tiled=True),
    )
    mine_keys = take_blocks(got_keys, my_slot)
    mine_values = take_blocks(got_values, my_slot)
    other_keys, other_values = (
        partner(as_sent(mine_keys), "ctx", 0).astype(mine_keys.dtype),
        partner(as_sent(mine_values), "ctx", 0).astype(mine_values.dtype),
    )
    first_keys = jnp.where(parity == 0, mine_keys, other_keys)
    second_keys = jnp.where(parity == 0, other_keys, mine_keys)
    first_values = jnp.where(parity == 0, mine_values, other_values)
    second_values = jnp.where(parity == 0, other_values, mine_values)
    live_keys = jnp.concatenate([first_keys, second_keys], axis=2)
    live_values = jnp.concatenate([first_values, second_values], axis=2)
    span_cols = TOPK * BLOCK
    live_keys = live_keys.reshape(kv_dev, span_cols, head_dim)
    live_values = live_values.reshape(kv_dev, span_cols, head_dim)
    all_keys = jnp.concatenate([live_keys, prev_keys, stretch_keys], axis=1)
    all_values = jnp.concatenate([live_values, prev_values, stretch_values], axis=1)
    query_rows = queries.reshape(kv_dev, q_per_kv * tok_dev, head_dim)
    step_rows = min(512, q_per_kv * tok_dev)
    columns = jnp.arange(span_cols + 2 * tok_dev, dtype=jnp.int32)

    def one_head(packed):
        q_head, k_head, v_head = packed
        q_steps = q_head.reshape(-1, step_rows, head_dim)
        starts = jnp.arange(q_steps.shape[0], dtype=jnp.int32) * step_rows

        def one_step(packed_block_step):
            q_block, first_row = packed_block_step
            position = (first_row + jnp.arange(step_rows, dtype=jnp.int32)) % tok_dev
            cache_part = columns[None, :] < span_cols
            earlier_part = (
                (columns[None, :] >= span_cols)
                & (columns[None, :] < span_cols + tok_dev)
                & (columns[None, :] - span_cols > position[:, None])
                & (ctx_index > 0)
            )
            own_part = (columns[None, :] >= span_cols + tok_dev) & (
                columns[None, :] - span_cols - tok_dev <= position[:, None]
            )
            return attend(q_block, k_head, v_head, cache_part | earlier_part | own_part)

        return lax.map(one_step, (q_steps, starts)).reshape(q_per_kv * tok_dev, head_dim)

    result = lax.map(one_head, (query_rows, all_keys, all_values))
    return result.reshape(kv_dev * q_per_kv, tok_dev, head_dim)


def solution(mesh):
    placed = (
        P(("head", "tp"), ("groups", "ctx"), None),
        P(("head", "tp"), ("groups", "ctx"), None),
        P(("head", "tp"), ("groups", "ctx"), None),
        P(("head", "tp"), ("groups", "ctx"), None),
        P(("head", "tp"), ("groups", "ctx"), None),
        P("groups", None, None),
        P("groups"),
    )
    return jax.shard_map(
        shards,
        mesh=mesh,
        in_specs=placed,
        out_specs=P(("head", "tp"), ("groups", "ctx"), None),
        check_vma=False,
    )
```

profile of v0, /device:TPU:0, one launch (start us, length us, event | category | flops | bytes accessed | tf_op | source)
XLA Modules:
  0.0 363.8 jit_solution(13856905821156815247)
XLA Ops:
  7.9 3.9 %gather_fusion.5 = bf16[32,256,128]{2,1,0:T(8,128)(2,1)} fusion(bf16[2,16,256,128]{3,2,1,0:T(8,128)(2,1)} %bitcast.67, s32[32]{0:T(128)S(1)} %reshape.259), kind=kCustom, calls=%fused_computation.5 | custom fusion | bytes 4194560 | tf_op jit(solution)/shard_map/vmap()/gather | solution.py:43
  11.9 3.2 broadcast_select_fusion
  16.7 6.4 %all-to-all-start = ((bf16[2,16,256,128]{3,2,0,1:T(8,128)(2,1)}), bf16[2,16,256,128]{3,2,0,1:T(8,128)(2,1)S(1)}, u32[]{:S(2)}, u32[]{:S(2)}) async-start(bf16[2,16,256,128]{3,2,0,1:T(8,128)(2,1)} %copy.18), calls=%async_computation | async-start | bytes 4194304 | tf_op jit(solution)/shard_map/all_to_all | solution.py:111
  23.1 3.1 copy.19
  26.2 45.1 %all-to-all-done = bf16[2,16,256,128]{3,2,0,1:T(8,128)(2,1)S(1)} async-done(((bf16[2,16,256,128]{3,2,0,1:T(8,128)(2,1)}), bf16[2,16,256,128]{3,2,0,1:T(8,128)(2,1)S(1)}, u32[]{:S(2)}, u32[]{:S(2)}) %all-to-all-start) | async-done | bytes 2097184 | tf_op jit(solution)/shard_map/all_to_all | solution.py:111
  71.3 4.5 %all-to-all-start.1 = ((bf16[2,16,256,128]{3,2,0,1:T(8,128)(2,1)}), bf16[2,16,256,128]{3,2,0,1:T(8,128)(2,1)}, u32[]{:S(2)}, u32[]{:S(2)}) async-start(bf16[2,16,256,128]{3,2,0,1:T(8,128)(2,1)} %copy.19), calls=%async_computation.1 | async-start | bytes 4194304 | tf_op jit(solution)/shard_map/all_to_all | solution.py:112
  80.5 43.2 %all-to-all-done.1 = bf16[2,16,256,128]{3,2,0,1:T(8,128)(2,1)} async-done(((bf16[2,16,256,128]{3,2,0,1:T(8,128)(2,1)}), bf16[2,16,256,128]{3,2,0,1:T(8,128)(2,1)}, u32[]{:S(2)}, u32[]{:S(2)}) %all-to-all-start.1) | async-done | bytes 2097184 | tf_op jit(solution)/shard_map/all_to_all | solution.py:112
  123.7 3.7 %gather_fusion.6 = bf16[32,256,128]{2,1,0:T(8,128)(2,1)} fusion(bf16[2,16,256,128]{3,2,0,1:T(8,128)(2,1)} %all-to-all-done.1, s32[32]{0:T(128)S(1)} %reshape.265), kind=kCustom, calls=%fused_computation.6 | custom fusion | bytes 4194560 | tf_op jit(solution)/shard_map/vmap()/gather | solution.py:43
  127.4 3.9 %collective-permute-start.3 = (bf16[2,256,128]{2,1,0:T(8,128)(2,1)S(1)}, bf16[2,256,128]{2,1,0:T(8,128)(2,1)S(1)}, u32[]{:S(2)}, u32[]{:S(2)}) collective-permute-start(bf16[2,256,128]{2,1,0:T(8,128)(2,1)S(1)} %copy-done.5), channel_id=1, source_target_pairs={{0,4},{4,8},{8,12},{1,5},{5,9},{9,13},{2,6},{6,10},{10,14},{3,7},{... | collective-permute-start | bytes 393224 | tf_op jit(solution)/shard_map/ppermute | solution.py:14
  131.4 2.6 collective-permute-start.1
  134.0 24.2 %collective-permute-done = bf16[2,16,256,128]{3,2,1,0:T(8,128)(2,1)} collective-permute-done((bf16[2,16,256,128]{3,2,1,0:T(8,128)(2,1)S(1)}, bf16[2,16,256,128]{3,2,1,0:T(8,128)(2,1)}, u32[]{:S(2)}, u32[]{:S(2)}) %collective-permute-start) | collective-permute-done | bytes 2097184 | tf_op jit(solution)/shard_map/ppermute | solution.py:28
  158.2 43.1 %collective-permute-done.2 = bf16[2,16,256,128]{3,2,1,0:T(8,128)(2,1)} collective-permute-done((bf16[2,16,256,128]{3,2,1,0:T(8,128)(2,1)}, bf16[2,16,256,128]{3,2,1,0:T(8,128)(2,1)}, u32[]{:S(2)}, u32[]{:S(2)}) %collective-permute-start.2) | collective-permute-done | bytes 2097184 | tf_op jit(solution)/shard_map/ppermute | solution.py:28
  201.3 3.1 broadcast_select_fusion.3
  204.9 10.0 %pad_maximum_fusion.1 = bf16[2,8704,128]{2,1,0:T(8,128)(2,1)} fusion(bf16[2,256,128]{2,1,0:T(8,128)(2,1)S(1)} %copy-done.5, bf16[2,256,128]{2,1,0:T(8,128)(2,1)S(1)} %collective-permute-done.3, bf16[2,8192,128]{2,1,0:T(8,128)(2,1)S(1)} %bitcast.56), kind=kLoop, calls=%fused_computation.36 | loop fusion | flops 13369344 | bytes 8912896 | tf_op jit(solution)/shard_map/concatenate | solution.py:130
  215.3 9.9 %pad_maximum_fusion = bf16[2,8704,128]{2,1,0:T(8,128)(2,1)} fusion(bf16[2,256,128]{2,1,0:T(8,128)(2,1)S(1)} %copy-done.6, bf16[2,256,128]{2,1,0:T(8,128)(2,1)S(1)} %collective-permute-done.1, bf16[2,8192,128]{2,1,0:T(8,128)(2,1)S(1)} %bitcast.57), kind=kLoop, calls=%fused_computation.35 | loop fusion | flops 13369344 | bytes 8912896 | tf_op jit(solution)/shard_map/concatenate | solution.py:129
  225.2 136.7 %while.49 = (s32[]{:T(128)}, bf16[2,1024,128]{2,1,0:T(8,128)(2,1)S(1)}, bf16[2,1024,128]{2,1,0:T(8,128)(2,1)S(1)}, bf16[2,8704,128]{2,1,0:T(8,128)(2,1)}, bf16[2...) while((s32[]{:T(128)}, ...), condition=%wide.region_10.11_spmd.clone.clone, body=%wide.region_5.10_spmd.clone.clone.sunk | while | flops 2344288768 | bytes 68473648 | solution.py:157
  225.2 3.9 %dynamic-slice_bitcast_fusion.3 = (bf16[8704,128]{1,0:T(8,128)(2,1)}, bf16[8704,128]{1,0:T(8,128)(2,1)}) fusion(bf16[2,8704,128]{2,1,0:T(8,128)(2,1)} %get-tuple-element.681, s32[]{:T(128)} %get-tuple-element.668, bf16[2,8704,128]{2,1,0:T(8,128)(2,1)} %get-tuple-element.680), kind=kLoop, calls=%fused_computation.30.clone.1 | loop fusion | bytes 8912900 | tf_op jit(solution)/shard_map/while/body/jit(dynamic_index_in_dim)/squeeze | solution.py:157
  229.2 64.4 %while.50 = (s32[]{:T(128)}, bf16[2,512,128]{2,1,0:T(8,128)(2,1)S(1)}, s32[8704]{0:T(1024)S(1)}, s32[2]{0:T(128)S(1)}, pred[]{:T(512)}, /*index=5*/bf16[2,512,12...) while((s32[]{:T(128)}, ...), condition=%wide.region_9.9_spmd.clone, body=%wide.region_6.8_spmd.clone.sunk | while | flops 2344288768 | bytes 58477172 | solution.py:155
  230.4 13.1 %fusion.43 = (f32[512]{0:T(512)S(1)}, f32[512,8704]{1,0:T(8,128)}) fusion(bf16[8704,128]{1,0:T(8,128)(2,1)} %get-tuple-element.656, bf16[2,512,128]{2,1,0:T(8,128)(2,1)S(1)} %get-tuple-element.655, s32[]{:T(128)} %get-tuple-element.641, s32[8704]{0:T(1024)S(1)} %get-tuple-element.625, pred[8704]{0:T(1024)(128)(4,1)S(1)} %get-tuple-element.626, ...), kind=kOutput, calls=%fused_computation.75.clone.1 | convolution fusion | flops 1185414656 | bytes 20290564 | tf_op jit(solution)/shard_map/while/body/eval_jaxpr/while/body/eval_jaxpr/rd,kd->rk/dot_general | solution.py:51
  243.5 8.5 %fusion.44 = f32[512]{0:T(512)S(1)} fusion(f32[512,8704]{1,0:T(8,128)} %get-tuple-element.630, f32[512]{0:T(512)S(1)} %get-tuple-element.631), kind=kLoop, calls=%fused_computation.10.clone.1 | loop fusion | flops 8912384 | bytes 17829888 | tf_op jit(solution)/shard_map/while/body/eval_jaxpr/while/body/eval_jaxpr/reduce_sum | solution.py:58
  252.1 9.3 %fusion.45 = bf16[2,512,128]{2,1,0:T(8,128)(2,1)S(1)} fusion(bf16[2,512,128]{2,1,0:T(8,128)(2,1)S(1)} %get-tuple-element.642, s32[]{:T(128)} %get-tuple-element.641, bf16[8704,128]{1,0:T(8,128)(2,1)} %get-tuple-element.657, f32[512,8704]{1,0:T(8,128)} %get-tuple-element.630, f32[512]{0:T(512)S(1)} %get-tuple-element.631, f32[512]{0:T(512)S(1)} %fusion.44), kind=kOutput, calls=%fused_computation.17.clone.1 | convolution fusion | flops 1149894656 | bytes 20189188 | tf_op jit(solution)/shard_map/while/body/eval_jaxpr/while/body/eval_jaxpr/rk,kd->rd/dot_general | solution.py:59
  262.6 13.1 %fusion.43 = (f32[512]{0:T(512)S(1)}, f32[512,8704]{1,0:T(8,128)}) fusion(bf16[8704,128]{1,0:T(8,128)(2,1)} %get-tuple-element.656, bf16[2,512,128]{2,1,0:T(8,128)(2,1)S(1)} %get-tuple-element.655, s32[]{:T(128)} %get-tuple-element.641, s32[8704]{0:T(1024)S(1)} %get-tuple-element.625, pred[8704]{0:T(1024)(128)(4,1)S(1)} %get-tuple-element.626, ...), kind=kOutput, calls=%fused_computation.75.clone.1 | convolution fusion | flops 1185414656 | bytes 20290564 | tf_op jit(solution)/shard_map/while/body/eval_jaxpr/while/body/eval_jaxpr/rd,kd->rk/dot_general | solution.py:51
  275.7 8.5 %fusion.44 = f32[512]{0:T(512)S(1)} fusion(f32[512,8704]{1,0:T(8,128)} %get-tuple-element.630, f32[512]{0:T(512)S(1)} %get-tuple-element.631), kind=kLoop, calls=%fused_computation.10.clone.1 | loop fusion | flops 8912384 | bytes 17829888 | tf_op jit(solution)/shard_map/while/body/eval_jaxpr/while/body/eval_jaxpr/reduce_sum | solution.py:58
  284.2 9.3 %fusion.45 = bf16[2,512,128]{2,1,0:T(8,128)(2,1)S(1)} fusion(bf16[2,512,128]{2,1,0:T(8,128)(2,1)S(1)} %get-tuple-element.642, s32[]{:T(128)} %get-tuple-element.641, bf16[8704,128]{1,0:T(8,128)(2,1)} %get-tuple-element.657, f32[512,8704]{1,0:T(8,128)} %get-tuple-element.630, f32[512]{0:T(512)S(1)} %get-tuple-element.631, f32[512]{0:T(512)S(1)} %fusion.44), kind=kOutput, calls=%fused_computation.17.clone.1 | convolution fusion | flops 1149894656 | bytes 20189188 | tf_op jit(solution)/shard_map/while/body/eval_jaxpr/while/body/eval_jaxpr/rk,kd->rd/dot_general | solution.py:59
  293.6 3.9 %dynamic-slice_bitcast_fusion.3 = (bf16[8704,128]{1,0:T(8,128)(2,1)}, bf16[8704,128]{1,0:T(8,128)(2,1)}) fusion(bf16[2,8704,128]{2,1,0:T(8,128)(2,1)} %get-tuple-element.681, s32[]{:T(128)} %get-tuple-element.668, bf16[2,8704,128]{2,1,0:T(8,128)(2,1)} %get-tuple-element.680), kind=kLoop, calls=%fused_computation.30.clone.1 | loop fusion | bytes 8912900 | tf_op jit(solution)/shard_map/while/body/jit(dynamic_index_in_dim)/squeeze | solution.py:157
  297.5 64.4 %while.50 = (s32[]{:T(128)}, bf16[2,512,128]{2,1,0:T(8,128)(2,1)S(1)}, s32[8704]{0:T(1024)S(1)}, s32[2]{0:T(128)S(1)}, pred[]{:T(512)}, /*index=5*/bf16[2,512,12...) while((s32[]{:T(128)}, ...), condition=%wide.region_9.9_spmd.clone, body=%wide.region_6.8_spmd.clone.sunk | while | flops 2344288768 | bytes 58477172 | solution.py:155
  298.8 13.1 %fusion.43 = (f32[512]{0:T(512)S(1)}, f32[512,8704]{1,0:T(8,128)}) fusion(bf16[8704,128]{1,0:T(8,128)(2,1)} %get-tuple-element.656, bf16[2,512,128]{2,1,0:T(8,128)(2,1)S(1)} %get-tuple-element.655, s32[]{:T(128)} %get-tuple-element.641, s32[8704]{0:T(1024)S(1)} %get-tuple-element.625, pred[8704]{0:T(1024)(128)(4,1)S(1)} %get-tuple-element.626, ...), kind=kOutput, calls=%fused_computation.75.clone.1 | convolution fusion | flops 1185414656 | bytes 20290564 | tf_op jit(solution)/shard_map/while/body/eval_jaxpr/while/body/eval_jaxpr/rd,kd->rk/dot_general | solution.py:51
  311.9 8.5 %fusion.44 = f32[512]{0:T(512)S(1)} fusion(f32[512,8704]{1,0:T(8,128)} %get-tuple-element.630, f32[512]{0:T(512)S(1)} %get-tuple-element.631), kind=kLoop, calls=%fused_computation.10.clone.1 | loop fusion | flops 8912384 | bytes 17829888 | tf_op jit(solution)/shard_map/while/body/eval_jaxpr/while/body/eval_jaxpr/reduce_sum | solution.py:58
  320.4 9.3 %fusion.45 = bf16[2,512,128]{2,1,0:T(8,128)(2,1)S(1)} fusion(bf16[2,512,128]{2,1,0:T(8,128)(2,1)S(1)} %get-tuple-element.642, s32[]{:T(128)} %get-tuple-element.641, bf16[8704,128]{1,0:T(8,128)(2,1)} %get-tuple-element.657, f32[512,8704]{1,0:T(8,128)} %get-tuple-element.630, f32[512]{0:T(512)S(1)} %get-tuple-element.631, f32[512]{0:T(512)S(1)} %fusion.44), kind=kOutput, calls=%fused_computation.17.clone.1 | convolution fusion | flops 1149894656 | bytes 20189188 | tf_op jit(solution)/shard_map/while/body/eval_jaxpr/while/body/eval_jaxpr/rk,kd->rd/dot_general | solution.py:59
  331.0 13.1 %fusion.43 = (f32[512]{0:T(512)S(1)}, f32[512,8704]{1,0:T(8,128)}) fusion(bf16[8704,128]{1,0:T(8,128)(2,1)} %get-tuple-element.656, bf16[2,512,128]{2,1,0:T(8,128)(2,1)S(1)} %get-tuple-element.655, s32[]{:T(128)} %get-tuple-element.641, s32[8704]{0:T(1024)S(1)} %get-tuple-element.625, pred[8704]{0:T(1024)(128)(4,1)S(1)} %get-tuple-element.626, ...), kind=kOutput, calls=%fused_computation.75.clone.1 | convolution fusion | flops 1185414656 | bytes 20290564 | tf_op jit(solution)/shard_map/while/body/eval_jaxpr/while/body/eval_jaxpr/rd,kd->rk/dot_general | solution.py:51
  344.1 8.5 %fusion.44 = f32[512]{0:T(512)S(1)} fusion(f32[512,8704]{1,0:T(8,128)} %get-tuple-element.630, f32[512]{0:T(512)S(1)} %get-tuple-element.631), kind=kLoop, calls=%fused_computation.10.clone.1 | loop fusion | flops 8912384 | bytes 17829888 | tf_op jit(solution)/shard_map/while/body/eval_jaxpr/while/body/eval_jaxpr/reduce_sum | solution.py:58
  352.6 9.3 %fusion.45 = bf16[2,512,128]{2,1,0:T(8,128)(2,1)S(1)} fusion(bf16[2,512,128]{2,1,0:T(8,128)(2,1)S(1)} %get-tuple-element.642, s32[]{:T(128)} %get-tuple-element.641, bf16[8704,128]{1,0:T(8,128)(2,1)} %get-tuple-element.657, f32[512,8704]{1,0:T(8,128)} %get-tuple-element.630, f32[512]{0:T(512)S(1)} %get-tuple-element.631, f32[512]{0:T(512)S(1)} %fusion.44), kind=kOutput, calls=%fused_computation.17.clone.1 | convolution fusion | flops 1149894656 | bytes 20189188 | tf_op jit(solution)/shard_map/while/body/eval_jaxpr/while/body/eval_jaxpr/rk,kd->rd/dot_general | solution.py:59
  (75 shorter events, 22.1 us)
Async XLA Ops:
  0.0 5.8 %copy-start = (bf16[2,4096,128]{2,1,0:T(8,128)(2,1)S(1)}, bf16[2,4096,128]{2,1,0:T(8,128)(2,1)}, u32[]{:S(2)}) copy-start(bf16[2,4096,128]{2,1,0:T(8,128)(2,1)} %param.19) | copy-start | bytes 6291460
  7.9 4.0 %copy-start.3 = (bf16[32,256,128]{2,1,0:T(8,128)(2,1)S(1)}, bf16[32,256,128]{2,1,0:T(8,128)(2,1)}, u32[]{:S(2)}) copy-start(bf16[32,256,128]{2,1,0:T(8,128)(2,1)} %gather_fusion.3) | copy-start | bytes 6291460
  16.7 54.6 %all-to-all-start = ((bf16[2,16,256,128]{3,2,0,1:T(8,128)(2,1)}), bf16[2,16,256,128]{3,2,0,1:T(8,128)(2,1)S(1)}, u32[]{:S(2)}, u32[]{:S(2)}) async-start(bf16[2,16,256,128]{3,2,0,1:T(8,128)(2,1)} %copy.18), calls=%async_computation | async-start | bytes 4194304 | tf_op jit(solution)/shard_map/all_to_all | solution.py:111
  71.3 4.5 %copy-start.2 = (bf16[2,16,256,128]{3,2,0,1:T(8,128)(2,1)}, bf16[2,16,256,128]{3,2,0,1:T(8,128)(2,1)S(1)}, u32[]{:S(2)}) copy-start(bf16[2,16,256,128]{3,2,0,1:T(8,128)(2,1)S(1)} %all-to-all-done) | copy-start | bytes 6291460
  71.3 52.4 %all-to-all-start.1 = ((bf16[2,16,256,128]{3,2,0,1:T(8,128)(2,1)}), bf16[2,16,256,128]{3,2,0,1:T(8,128)(2,1)}, u32[]{:S(2)}, u32[]{:S(2)}) async-start(bf16[2,16,256,128]{3,2,0,1:T(8,128)(2,1)} %copy.19), calls=%async_computation.1 | async-start | bytes 4194304 | tf_op jit(solution)/shard_map/all_to_all | solution.py:112
  75.9 51.5 %copy-start.5 = (bf16[2,256,128]{2,1,0:T(8,128)(2,1)S(1)}, bf16[2,256,128]{2,1,0:T(8,128)(2,1)}, u32[]{:S(2)}) copy-start(bf16[2,256,128]{2,1,0:T(8,128)(2,1)} %param.18) | copy-start | bytes 393220
  75.9 55.5 %copy-start.6 = (bf16[2,256,128]{2,1,0:T(8,128)(2,1)S(1)}, bf16[2,256,128]{2,1,0:T(8,128)(2,1)}, u32[]{:S(2)}) copy-start(bf16[2,256,128]{2,1,0:T(8,128)(2,1)} %param.17) | copy-start | bytes 393220
  78.5 79.7 %collective-permute-start = (bf16[2,16,256,128]{3,2,1,0:T(8,128)(2,1)S(1)}, bf16[2,16,256,128]{3,2,1,0:T(8,128)(2,1)}, u32[]{:S(2)}, u32[]{:S(2)}) collective-permute-start(bf16[2,16,256,128]{3,2,1,0:T(8,128)(2,1)S(1)} %bitcast.58), channel_id=1, source_target_pairs={{0,4},{4,0},{8,12},{12,8},{1,5},{5,1},{9,13},{13,9},{2,6},{6,2},{1... | collective-permute-start | bytes 6291464 | tf_op jit(solution)/shard_map/ppermute | solution.py:28
  127.4 73.9 %collective-permute-start.2 = (bf16[2,16,256,128]{3,2,1,0:T(8,128)(2,1)}, bf16[2,16,256,128]{3,2,1,0:T(8,128)(2,1)}, u32[]{:S(2)}, u32[]{:S(2)}) collective-permute-start(bf16[2,16,256,128]{3,2,1,0:T(8,128)(2,1)} %bitcast.60), channel_id=1, source_target_pairs={{0,4},{4,0},{8,12},{12,8},{1,5},{5,1},{9,13},{13,9},{2,6},{6,2},{1... | collective-permute-start | bytes 6291464 | tf_op jit(solution)/shard_map/ppermute | solution.py:28
  127.4 77.5 %collective-permute-start.3 = (bf16[2,256,128]{2,1,0:T(8,128)(2,1)S(1)}, bf16[2,256,128]{2,1,0:T(8,128)(2,1)S(1)}, u32[]{:S(2)}, u32[]{:S(2)}) collective-permute-start(bf16[2,256,128]{2,1,0:T(8,128)(2,1)S(1)} %copy-done.5), channel_id=1, source_target_pairs={{0,4},{4,8},{8,12},{1,5},{5,9},{9,13},{2,6},{6,10},{10,14},{3,7},{... | collective-permute-start | bytes 393224 | tf_op jit(solution)/shard_map/ppermute | solution.py:14
  131.4 83.9 %collective-permute-start.1 = (bf16[2,256,128]{2,1,0:T(8,128)(2,1)S(1)}, bf16[2,256,128]{2,1,0:T(8,128)(2,1)S(1)}, u32[]{:S(2)}, u32[]{:S(2)}) collective-permute-start(bf16[2,256,128]{2,1,0:T(8,128)(2,1)S(1)} %copy-done.6), channel_id=1, source_target_pairs={{0,4},{4,8},{8,12},{1,5},{5,9},{9,13},{2,6},{6,10},{10,14},{3,7},{... | collective-permute-start | bytes 393224 | tf_op jit(solution)/shard_map/ppermute | solution.py:14
  215.3 9.9 %copy-start.4 = (bf16[8,256,128]{2,1,0:T(8,128)(2,1)S(1)}, bf16[8,256,128]{2,1,0:T(8,128)(2,1)}, u32[]{:S(2)}) copy-start(bf16[8,256,128]{2,1,0:T(8,128)(2,1)} %param.16) | copy-start | bytes 1572868
  362.0 0.8 copy-start.7
  362.0 1.8 copy-start.1
where the time goes:
time: 365 us; the launch traced here: 364 us
  waiting for transfers between devices  156 us (43%)
  matrix products  89.4 us (24%)
  other arithmetic  67.8 us (19%)
  local copies, waits for them, and re-layouts  31.2 us (9%)
  starting transfers between devices  19.4 us (5%)
    ppermute x2, waiting for transfers between devices, partner(): return lax.ppermute(value, axis, pairs)  67.3 us
    dot_general x4, matrix products, attend(): jnp.einsum('rd,kd->rk', query_rows, all_keys, preferred_element_type=jnp....  52.3 us
    all_to_all x1, waiting for transfers between devices, shards(): lax.all_to_all(sent_keys, 'ctx', split_axis=1, concat_axis=1, tiled=True)  45.1 us
    all_to_all x1, waiting for transfers between devices, shards(): lax.all_to_all(sent_values, 'ctx', split_axis=1, concat_axis=1, tiled=True)  43.2 us
    dot_general x4, matrix products, attend(): jnp.einsum('rk,kd->rd', weights.astype(jnp.bfloat16), all_values, preferr...  37.1 us
    reduce_sum x4, other arithmetic, attend(): weight_sum = jnp.sum(weights, axis=-1, keepdims=True)  34.2 us
    gather x6, local copies, waits for them, and re-layouts, pick_rows(): return source[indices]  12.5 us
    concatenate x1, other arithmetic, shards(): jnp.concatenate([live_values, prev_values, stretch_values], axis=1)  9.97 us
  transfers between devices with their start and end apart: 6, of which 4 were waited for; matrix products, arithmetic and copies ran while one was open for 6% of the time, Pallas kernels for 0%

commit v1 on v0

--- a/solution.py
+++ b/solution.py
@@ -6,6 +6,29 @@
 
 BLOCK = 512
 TOPK = 16
+
+
+def cut_along(shard, dim, peers):
+    shape = shard.shape
+    blocks = shard.reshape(*shape[:dim], peers, shape[dim] // peers, *shape[dim + 1 :])
+    return jnp.moveaxis(blocks, dim, 0)
+
+
+def in_order(blocks, dim):
+    lengths = list(blocks.shape[1:])
+    lengths[dim] *= blocks.shape[0]
+    return jnp.moveaxis(blocks, 0, dim).reshape(lengths)
+
+
+def pairwise_exchange(value, axis, split_dim, concat_dim):
+    peers, index = (lax.axis_size(axis), lax.axis_index(axis))
+    parts = cut_along(value, split_dim, peers)
+    outs = [parts[index]]
+    for step in range(1, peers):
+        sent = parts[index ^ step]
+        outs.append(lax.ppermute(sent, axis, [(i, i ^ step) for i in range(peers)]))
+    parts = jnp.stack(outs)[index ^ jnp.arange(peers)]
+    return in_order(parts, concat_dim)
 
 
 def shifted(value, axis, by):
@@ -109,7 +132,7 @@
     ).astype(jnp.bfloat16)
     got_keys, got_values = (
         lax.all_to_all(sent_keys, "ctx", split_axis=1, concat_axis=1, tiled=True),
-        lax.all_to_all(sent_values, "ctx", split_axis=1, concat_axis=1, tiled=True),
+        pairwise_exchange(sent_values, "ctx", 1, 1),
     )
     mine_keys = take_blocks(got_keys, my_slot)
     mine_values = take_blocks(got_values, my_slot)

time: 365 us -> 375 us (1.027)
  starting transfers between devices: 19.4 us -> 27.6 us
    ppermute x0 -> x3, waiting for transfers between devices: none -> 75.3 us  [pairwise_exchange(): outs.append(lax.ppermute(sent, axis, [(i, i ^ step) for i in range(peers)]))]
    all_to_all x1, waiting for transfers between devices: 45.1 us -> 0.01 us  [shards(): lax.all_to_all(sent_keys, 'ctx', split_axis=1, concat_axis=1, tiled=True)]
    all_to_all x1 -> x0, waiting for transfers between devices: 43.2 us -> none  [shards(): lax.all_to_all(sent_values, 'ctx', split_axis=1, concat_axis=1, tiled=True)]
    ppermute x2, waiting for transfers between devices: 67.3 us -> 80.7 us  [partner(): return lax.ppermute(value, axis, pairs)]
    ppermute x2, starting transfers between devices: 2.02 us -> 10.2 us  [partner(): return lax.ppermute(value, axis, pairs)]
    ppermute x0 -> x3, starting transfers between devices: none -> 4.53 us  [pairwise_exchange(): outs.append(lax.ppermute(sent, axis, [(i, i ^ step) for i in range(peers)]))]
    all_to_all x1 -> x0, starting transfers between devices: 4.47 us -> none  [shards(): lax.all_to_all(sent_values, 'ctx', split_axis=1, concat_axis=1, tiled=True)]
  transfers between devices with their start and end apart: 6 -> 8, of which waited for: 4 -> 4; matrix products, arithmetic and copies ran while one was open for 6% -> 8% of each run, Pallas kernels for 0% -> 0%
where the time goes in v1:
time: 375 us
  waiting for transfers between devices  156 us (42%)
  matrix products  89.4 us (24%)
  other arithmetic  68.1 us (18%)
  local copies, waits for them, and re-layouts  32.9 us (9%)
  starting transfers between devices  27.6 us (7%)
    ppermute x2, waiting for transfers between devices, partner(): return lax.ppermute(value, axis, pairs)  80.7 us
    ppermute x3, waiting for transfers between devices, pairwise_exchange(): outs.append(lax.ppermute(sent, axis, [(i, i ^ step) for i in range(peers)]))  75.3 us
    dot_general x4, matrix products, attend(): jnp.einsum('rd,kd->rk', query_rows, all_keys, preferred_element_type=jnp....  52.3 us
    dot_general x4, matrix products, attend(): jnp.einsum('rk,kd->rd', weights.astype(jnp.bfloat16), all_values, preferr...  37.1 us
    reduce_sum x4, other arithmetic, attend(): weight_sum = jnp.sum(weights, axis=-1, keepdims=True)  34.2 us
    gather x6, local copies, waits for them, and re-layouts, pick_rows(): return source[indices]  11.1 us
    ppermute x2, starting transfers between devices, partner(): return lax.ppermute(value, axis, pairs)  10.2 us
    concatenate x1, other arithmetic, shards(): jnp.concatenate([live_values, prev_values, stretch_values], axis=1)  9.97 us
  transfers between devices with their start and end apart: 8, of which 4 were waited for; matrix products, arithmetic and copies ran while one was open for 8% of the time, Pallas kernels for 0%

profile of v1, /device:TPU:0, one launch (start us, length us, event | category | flops | bytes accessed | tf_op | source)
XLA Modules:
  0.0 374.5 jit_solution(12109127555479118434)
XLA Ops:
  11.4 6.4 %all-to-all-start = ((bf16[2,16,256,128]{3,2,0,1:T(8,128)(2,1)}), bf16[2,16,256,128]{3,2,0,1:T(8,128)(2,1)}, u32[]{:S(2)}, u32[]{:S(2)}) async-start(bf16[2,16,256,128]{3,2,0,1:T(8,128)(2,1)} %copy.22), calls=%async_computation | async-start | bytes 4194304 | tf_op jit(solution)/shard_map/all_to_all | solution.py:134
  17.8 2.5 gather_fusion.6
  25.4 38.7 %collective-permute-done.2 = bf16[2,4,256,128]{3,2,1,0:T(8,128)(2,1)S(1)} collective-permute-done((bf16[2,4,256,128]{3,2,1,0:T(8,128)(2,1)S(1)}, bf16[2,4,256,128]{3,2,1,0:T(8,128)(2,1)S(1)}, u32[]{:S(2)}, u32[]{:S(2)}) %collective-permute-start.2) | collective-permute-done | bytes 524320 | tf_op jit(solution)/shard_map/ppermute | solution.py:29
  64.0 36.6 %collective-permute-done.3 = bf16[2,4,256,128]{3,2,1,0:T(8,128)(2,1)S(1)} collective-permute-done((bf16[2,4,256,128]{3,2,1,0:T(8,128)(2,1)S(1)}, bf16[2,4,256,128]{3,2,1,0:T(8,128)(2,1)S(1)}, u32[]{:S(2)}, u32[]{:S(2)}) %collective-permute-start.3) | collective-permute-done | bytes 524320 | tf_op jit(solution)/shard_map/ppermute | solution.py:29
  105.0 3.2 copy.24
  108.2 2.5 gather_fusion.7
  110.8 10.2 %collective-permute-start.5 = (bf16[2,16,256,128]{3,2,1,0:T(8,128)(2,1)S(1)}, bf16[2,16,256,128]{3,2,1,0:T(8,128)(2,1)}, u32[]{:S(2)}, u32[]{:S(2)}) collective-permute-start(bf16[2,16,256,128]{3,2,1,0:T(8,128)(2,1)S(1)} %bitcast.77), channel_id=1, source_target_pairs={{0,4},{4,0},{8,12},{12,8},{1,5},{5,1},{9,13},{13,9},{2,6},{6,2},{1... | collective-permute-start | bytes 6291464 | tf_op jit(solution)/shard_map/ppermute | solution.py:51
  121.0 3.7 gather_fusion.5
  124.7 3.9 %collective-permute-start.6 = (bf16[2,256,128]{2,1,0:T(8,128)(2,1)S(1)}, bf16[2,256,128]{2,1,0:T(8,128)(2,1)S(1)}, u32[]{:S(2)}, u32[]{:S(2)}) collective-permute-start(bf16[2,256,128]{2,1,0:T(8,128)(2,1)S(1)} %copy-done.4), channel_id=1, source_target_pairs={{0,4},{4,8},{8,12},{1,5},{5,9},{9,13},{2,6},{6,10},{10,14},{3,7},{... | collective-permute-start | bytes 393224 | tf_op jit(solution)/shard_map/ppermute | solution.py:37
  128.6 2.7 collective-permute-start.1
  131.3 36.2 %collective-permute-done.5 = bf16[2,16,256,128]{3,2,1,0:T(8,128)(2,1)} collective-permute-done((bf16[2,16,256,128]{3,2,1,0:T(8,128)(2,1)S(1)}, bf16[2,16,256,128]{3,2,1,0:T(8,128)(2,1)}, u32[]{:S(2)}, u32[]{:S(2)}) %collective-permute-start.5) | collective-permute-done | bytes 2097184 | tf_op jit(solution)/shard_map/ppermute | solution.py:51
  167.6 44.5 %collective-permute-done = bf16[2,16,256,128]{3,2,1,0:T(8,128)(2,1)} collective-permute-done((bf16[2,16,256,128]{3,2,1,0:T(8,128)(2,1)}, bf16[2,16,256,128]{3,2,1,0:T(8,128)(2,1)}, u32[]{:S(2)}, u32[]{:S(2)}) %collective-permute-start) | collective-permute-done | bytes 2097184 | tf_op jit(solution)/shard_map/ppermute | solution.py:51
  212.0 3.1 broadcast_select_fusion.3
  215.6 10.0 %pad_maximum_fusion.1 = bf16[2,8704,128]{2,1,0:T(8,128)(2,1)} fusion(bf16[2,256,128]{2,1,0:T(8,128)(2,1)S(1)} %copy-done.4, bf16[2,256,128]{2,1,0:T(8,128)(2,1)S(1)} %collective-permute-done.6, bf16[2,8192,128]{2,1,0:T(8,128)(2,1)S(1)} %bitcast.75), kind=kLoop, calls=%fused_computation.37 | loop fusion | flops 13369344 | bytes 8912896 | tf_op jit(solution)/shard_map/concatenate | solution.py:153
  226.1 9.9 %pad_maximum_fusion = bf16[2,8704,128]{2,1,0:T(8,128)(2,1)} fusion(bf16[2,256,128]{2,1,0:T(8,128)(2,1)S(1)} %copy-done.5, bf16[2,256,128]{2,1,0:T(8,128)(2,1)S(1)} %collective-permute-done.1, bf16[2,8192,128]{2,1,0:T(8,128)(2,1)S(1)} %bitcast.76), kind=kLoop, calls=%fused_computation.36 | loop fusion | flops 13369344 | bytes 8912896 | tf_op jit(solution)/shard_map/concatenate | solution.py:152
  236.0 136.7 %while.49 = (s32[]{:T(128)}, bf16[2,1024,128]{2,1,0:T(8,128)(2,1)S(1)}, bf16[2,1024,128]{2,1,0:T(8,128)(2,1)S(1)}, bf16[2,8704,128]{2,1,0:T(8,128)(2,1)}, bf16[2...) while((s32[]{:T(128)}, ...), condition=%wide.region_10.11_spmd.clone.clone, body=%wide.region_5.10_spmd.clone.clone.sunk | while | flops 2344288768 | bytes 68473648 | solution.py:180
  236.0 3.9 %dynamic-slice_bitcast_fusion.7 = (bf16[8704,128]{1,0:T(8,128)(2,1)}, bf16[8704,128]{1,0:T(8,128)(2,1)}) fusion(bf16[2,8704,128]{2,1,0:T(8,128)(2,1)} %get-tuple-element.683, s32[]{:T(128)} %get-tuple-element.670, bf16[2,8704,128]{2,1,0:T(8,128)(2,1)} %get-tuple-element.682), kind=kLoop, calls=%fused_computation.31.clone.1 | loop fusion | bytes 8912900 | tf_op jit(solution)/shard_map/while/body/jit(dynamic_index_in_dim)/squeeze | solution.py:180
  239.9 64.4 %while.50 = (s32[]{:T(128)}, bf16[2,512,128]{2,1,0:T(8,128)(2,1)S(1)}, s32[8704]{0:T(1024)S(1)}, s32[2]{0:T(128)S(1)}, pred[]{:T(512)}, /*index=5*/bf16[2,512,12...) while((s32[]{:T(128)}, ...), condition=%wide.region_9.9_spmd.clone, body=%wide.region_6.8_spmd.clone.sunk | while | flops 2344288768 | bytes 58477172 | solution.py:178
  241.2 13.1 %fusion.44 = (f32[512]{0:T(512)S(1)}, f32[512,8704]{1,0:T(8,128)}) fusion(bf16[8704,128]{1,0:T(8,128)(2,1)} %get-tuple-element.658, bf16[2,512,128]{2,1,0:T(8,128)(2,1)S(1)} %get-tuple-element.657, s32[]{:T(128)} %get-tuple-element.643, s32[8704]{0:T(1024)S(1)} %get-tuple-element.627, pred[8704]{0:T(1024)(128)(4,1)S(1)} %get-tuple-element.628, ...), kind=kOutput, calls=%fused_computation.87.clone.1 | convolution fusion | flops 1185414656 | bytes 20290564 | tf_op jit(solution)/shard_map/while/body/eval_jaxpr/while/body/eval_jaxpr/rd,kd->rk/dot_general | solution.py:74
  254.3 8.5 %fusion.45 = f32[512]{0:T(512)S(1)} fusion(f32[512,8704]{1,0:T(8,128)} %get-tuple-element.632, f32[512]{0:T(512)S(1)} %get-tuple-element.633), kind=kLoop, calls=%fused_computation.11.clone.1 | loop fusion | flops 8912384 | bytes 17829888 | tf_op jit(solution)/shard_map/while/body/eval_jaxpr/while/body/eval_jaxpr/reduce_sum | solution.py:81
  262.8 9.3 %fusion.46 = bf16[2,512,128]{2,1,0:T(8,128)(2,1)S(1)} fusion(bf16[2,512,128]{2,1,0:T(8,128)(2,1)S(1)} %get-tuple-element.644, s32[]{:T(128)} %get-tuple-element.643, bf16[8704,128]{1,0:T(8,128)(2,1)} %get-tuple-element.659, f32[512,8704]{1,0:T(8,128)} %get-tuple-element.632, f32[512]{0:T(512)S(1)} %get-tuple-element.633, f32[512]{0:T(512)S(1)} %fusion.45), kind=kOutput, calls=%fused_computation.18.clone.1 | convolution fusion | flops 1149894656 | bytes 20189188 | tf_op jit(solution)/shard_map/while/body/eval_jaxpr/while/body/eval_jaxpr/rk,kd->rd/dot_general | solution.py:82
  273.4 13.1 %fusion.44 = (f32[512]{0:T(512)S(1)}, f32[512,8704]{1,0:T(8,128)}) fusion(bf16[8704,128]{1,0:T(8,128)(2,1)} %get-tuple-element.658, bf16[2,512,128]{2,1,0:T(8,128)(2,1)S(1)} %get-tuple-element.657, s32[]{:T(128)} %get-tuple-element.643, s32[8704]{0:T(1024)S(1)} %get-tuple-element.627, pred[8704]{0:T(1024)(128)(4,1)S(1)} %get-tuple-element.628, ...), kind=kOutput, calls=%fused_computation.87.clone.1 | convolution fusion | flops 1185414656 | bytes 20290564 | tf_op jit(solution)/shard_map/while/body/eval_jaxpr/while/body/eval_jaxpr/rd,kd->rk/dot_general | solution.py:74
  286.5 8.5 %fusion.45 = f32[512]{0:T(512)S(1)} fusion(f32[512,8704]{1,0:T(8,128)} %get-tuple-element.632, f32[512]{0:T(512)S(1)} %get-tuple-element.633), kind=kLoop, calls=%fused_computation.11.clone.1 | loop fusion | flops 8912384 | bytes 17829888 | tf_op jit(solution)/shard_map/while/body/eval_jaxpr/while/body/eval_jaxpr/reduce_sum | solution.py:81
  295.0 9.3 %fusion.46 = bf16[2,512,128]{2,1,0:T(8,128)(2,1)S(1)} fusion(bf16[2,512,128]{2,1,0:T(8,128)(2,1)S(1)} %get-tuple-element.644, s32[]{:T(128)} %get-tuple-element.643, bf16[8704,128]{1,0:T(8,128)(2,1)} %get-tuple-element.659, f32[512,8704]{1,0:T(8,128)} %get-tuple-element.632, f32[512]{0:T(512)S(1)} %get-tuple-element.633, f32[512]{0:T(512)S(1)} %fusion.45), kind=kOutput, calls=%fused_computation.18.clone.1 | convolution fusion | flops 1149894656 | bytes 20189188 | tf_op jit(solution)/shard_map/while/body/eval_jaxpr/while/body/eval_jaxpr/rk,kd->rd/dot_general | solution.py:82
  304.4 3.9 %dynamic-slice_bitcast_fusion.7 = (bf16[8704,128]{1,0:T(8,128)(2,1)}, bf16[8704,128]{1,0:T(8,128)(2,1)}) fusion(bf16[2,8704,128]{2,1,0:T(8,128)(2,1)} %get-tuple-element.683, s32[]{:T(128)} %get-tuple-element.670, bf16[2,8704,128]{2,1,0:T(8,128)(2,1)} %get-tuple-element.682), kind=kLoop, calls=%fused_computation.31.clone.1 | loop fusion | bytes 8912900 | tf_op jit(solution)/shard_map/while/body/jit(dynamic_index_in_dim)/squeeze | solution.py:180
  308.3 64.4 %while.50 = (s32[]{:T(128)}, bf16[2,512,128]{2,1,0:T(8,128)(2,1)S(1)}, s32[8704]{0:T(1024)S(1)}, s32[2]{0:T(128)S(1)}, pred[]{:T(512)}, /*index=5*/bf16[2,512,12...) while((s32[]{:T(128)}, ...), condition=%wide.region_9.9_spmd.clone, body=%wide.region_6.8_spmd.clone.sunk | while | flops 2344288768 | bytes 58477172 | solution.py:178
  309.6 13.1 %fusion.44 = (f32[512]{0:T(512)S(1)}, f32[512,8704]{1,0:T(8,128)}) fusion(bf16[8704,128]{1,0:T(8,128)(2,1)} %get-tuple-element.658, bf16[2,512,128]{2,1,0:T(8,128)(2,1)S(1)} %get-tuple-element.657, s32[]{:T(128)} %get-tuple-element.643, s32[8704]{0:T(1024)S(1)} %get-tuple-element.627, pred[8704]{0:T(1024)(128)(4,1)S(1)} %get-tuple-element.628, ...), kind=kOutput, calls=%fused_computation.87.clone.1 | convolution fusion | flops 1185414656 | bytes 20290564 | tf_op jit(solution)/shard_map/while/body/eval_jaxpr/while/body/eval_jaxpr/rd,kd->rk/dot_general | solution.py:74
  322.7 8.5 %fusion.45 = f32[512]{0:T(512)S(1)} fusion(f32[512,8704]{1,0:T(8,128)} %get-tuple-element.632, f32[512]{0:T(512)S(1)} %get-tuple-element.633), kind=kLoop, calls=%fused_computation.11.clone.1 | loop fusion | flops 8912384 | bytes 17829888 | tf_op jit(solution)/shard_map/while/body/eval_jaxpr/while/body/eval_jaxpr/reduce_sum | solution.py:81
  331.2 9.3 %fusion.46 = bf16[2,512,128]{2,1,0:T(8,128)(2,1)S(1)} fusion(bf16[2,512,128]{2,1,0:T(8,128)(2,1)S(1)} %get-tuple-element.644, s32[]{:T(128)} %get-tuple-element.643, bf16[8704,128]{1,0:T(8,128)(2,1)} %get-tuple-element.659, f32[512,8704]{1,0:T(8,128)} %get-tuple-element.632, f32[512]{0:T(512)S(1)} %get-tuple-element.633, f32[512]{0:T(512)S(1)} %fusion.45), kind=kOutput, calls=%fused_computation.18.clone.1 | convolution fusion | flops 1149894656 | bytes 20189188 | tf_op jit(solution)/shard_map/while/body/eval_jaxpr/while/body/eval_jaxpr/rk,kd->rd/dot_general | solution.py:82
  341.8 13.1 %fusion.44 = (f32[512]{0:T(512)S(1)}, f32[512,8704]{1,0:T(8,128)}) fusion(bf16[8704,128]{1,0:T(8,128)(2,1)} %get-tuple-element.658, bf16[2,512,128]{2,1,0:T(8,128)(2,1)S(1)} %get-tuple-element.657, s32[]{:T(128)} %get-tuple-element.643, s32[8704]{0:T(1024)S(1)} %get-tuple-element.627, pred[8704]{0:T(1024)(128)(4,1)S(1)} %get-tuple-element.628, ...), kind=kOutput, calls=%fused_computation.87.clone.1 | convolution fusion | flops 1185414656 | bytes 20290564 | tf_op jit(solution)/shard_map/while/body/eval_jaxpr/while/body/eval_jaxpr/rd,kd->rk/dot_general | solution.py:74
  354.8 8.5 %fusion.45 = f32[512]{0:T(512)S(1)} fusion(f32[512,8704]{1,0:T(8,128)} %get-tuple-element.632, f32[512]{0:T(512)S(1)} %get-tuple-element.633), kind=kLoop, calls=%fused_computation.11.clone.1 | loop fusion | flops 8912384 | bytes 17829888 | tf_op jit(solution)/shard_map/while/body/eval_jaxpr/while/body/eval_jaxpr/reduce_sum | solution.py:81
  363.4 9.3 %fusion.46 = bf16[2,512,128]{2,1,0:T(8,128)(2,1)S(1)} fusion(bf16[2,512,128]{2,1,0:T(8,128)(2,1)S(1)} %get-tuple-element.644, s32[]{:T(128)} %get-tuple-element.643, bf16[8704,128]{1,0:T(8,128)(2,1)} %get-tuple-element.659, f32[512,8704]{1,0:T(8,128)} %get-tuple-element.632, f32[512]{0:T(512)S(1)} %get-tuple-element.633, f32[512]{0:T(512)S(1)} %fusion.45), kind=kOutput, calls=%fused_computation.18.clone.1 | convolution fusion | flops 1149894656 | bytes 20189188 | tf_op jit(solution)/shard_map/while/body/eval_jaxpr/while/body/eval_jaxpr/rk,kd->rd/dot_general | solution.py:82
  (83 shorter events, 28.7 us)
Async XLA Ops:
  0.0 5.9 %copy-start = (bf16[2,4096,128]{2,1,0:T(8,128)(2,1)S(1)}, bf16[2,4096,128]{2,1,0:T(8,128)(2,1)}, u32[]{:S(2)}) copy-start(bf16[2,4096,128]{2,1,0:T(8,128)(2,1)} %param.19) | copy-start | bytes 6291460
  11.4 109.6 %all-to-all-start = ((bf16[2,16,256,128]{3,2,0,1:T(8,128)(2,1)}), bf16[2,16,256,128]{3,2,0,1:T(8,128)(2,1)}, u32[]{:S(2)}, u32[]{:S(2)}) async-start(bf16[2,16,256,128]{3,2,0,1:T(8,128)(2,1)} %copy.22), calls=%async_computation | async-start | bytes 4194304 | tf_op jit(solution)/shard_map/all_to_all | solution.py:134
  20.7 43.3 %collective-permute-start.2 = (bf16[2,4,256,128]{3,2,1,0:T(8,128)(2,1)S(1)}, bf16[2,4,256,128]{3,2,1,0:T(8,128)(2,1)S(1)}, u32[]{:S(2)}, u32[]{:S(2)}) collective-permute-start(bf16[2,4,256,128]{3,2,1,0:T(8,128)(2,1)S(1)} %get-tuple-element.506), channel_id=1, source_target_pairs={{0,4},{4,0},{8,12},{12,8},{1,5},{5,1},{9,13},{13,9},{2,6},{6,2},{1... | collective-permute-start | bytes 1572872 | tf_op jit(solution)/shard_map/ppermute | solution.py:29
  22.8 77.8 %collective-permute-start.3 = (bf16[2,4,256,128]{3,2,1,0:T(8,128)(2,1)S(1)}, bf16[2,4,256,128]{3,2,1,0:T(8,128)(2,1)S(1)}, u32[]{:S(2)}, u32[]{:S(2)}) collective-permute-start(bf16[2,4,256,128]{3,2,1,0:T(8,128)(2,1)S(1)} %get-tuple-element.505), channel_id=1, source_target_pairs={{0,8},{4,12},{8,0},{12,4},{1,9},{5,13},{9,1},{13,5},{2,10},{6,14},... | collective-permute-start | bytes 1572872 | tf_op jit(solution)/shard_map/ppermute | solution.py:29
  25.2 75.5 %collective-permute-start.4 = (bf16[2,4,256,128]{3,2,1,0:T(8,128)(2,1)S(1)}, bf16[2,4,256,128]{3,2,1,0:T(8,128)(2,1)}, u32[]{:S(2)}, u32[]{:S(2)}) collective-permute-start(bf16[2,4,256,128]{3,2,1,0:T(8,128)(2,1)S(1)} %get-tuple-element.504), channel_id=1, source_target_pairs={{0,12},{4,8},{8,4},{12,0},{1,13},{5,9},{9,5},{13,1},{2,14},{6,10},... | collective-permute-start | bytes 1572872 | tf_op jit(solution)/shard_map/ppermute | solution.py:29
  100.7 0.8 copy-start.3
  110.8 14.0 %copy-start.4 = (bf16[2,256,128]{2,1,0:T(8,128)(2,1)S(1)}, bf16[2,256,128]{2,1,0:T(8,128)(2,1)}, u32[]{:S(2)}) copy-start(bf16[2,256,128]{2,1,0:T(8,128)(2,1)} %param.18) | copy-start | bytes 393220
  110.8 17.9 %copy-start.5 = (bf16[2,256,128]{2,1,0:T(8,128)(2,1)S(1)}, bf16[2,256,128]{2,1,0:T(8,128)(2,1)}, u32[]{:S(2)}) copy-start(bf16[2,256,128]{2,1,0:T(8,128)(2,1)} %param.17) | copy-start | bytes 393220
  110.8 56.8 %collective-permute-start.5 = (bf16[2,16,256,128]{3,2,1,0:T(8,128)(2,1)S(1)}, bf16[2,16,256,128]{3,2,1,0:T(8,128)(2,1)}, u32[]{:S(2)}, u32[]{:S(2)}) collective-permute-start(bf16[2,16,256,128]{3,2,1,0:T(8,128)(2,1)S(1)} %bitcast.77), channel_id=1, source_target_pairs={{0,4},{4,0},{8,12},{12,8},{1,5},{5,1},{9,13},{13,9},{2,6},{6,2},{1... | collective-permute-start | bytes 6291464 | tf_op jit(solution)/shard_map/ppermute | solution.py:51
  124.7 87.3 %collective-permute-start = (bf16[2,16,256,128]{3,2,1,0:T(8,128)(2,1)}, bf16[2,16,256,128]{3,2,1,0:T(8,128)(2,1)}, u32[]{:S(2)}, u32[]{:S(2)}) collective-permute-start(bf16[2,16,256,128]{3,2,1,0:T(8,128)(2,1)} %bitcast.79), channel_id=1, source_target_pairs={{0,4},{4,0},{8,12},{12,8},{1,5},{5,1},{9,13},{13,9},{2,6},{6,2},{1... | collective-permute-start | bytes 6291464 | tf_op jit(solution)/shard_map/ppermute | solution.py:51
  124.7 90.9 %collective-permute-start.6 = (bf16[2,256,128]{2,1,0:T(8,128)(2,1)S(1)}, bf16[2,256,128]{2,1,0:T(8,128)(2,1)S(1)}, u32[]{:S(2)}, u32[]{:S(2)}) collective-permute-start(bf16[2,256,128]{2,1,0:T(8,128)(2,1)S(1)} %copy-done.4), channel_id=1, source_target_pairs={{0,4},{4,8},{8,12},{1,5},{5,9},{9,13},{2,6},{6,10},{10,14},{3,7},{... | collective-permute-start | bytes 393224 | tf_op jit(solution)/shard_map/ppermute | solution.py:37
  128.6 97.4 %collective-permute-start.1 = (bf16[2,256,128]{2,1,0:T(8,128)(2,1)S(1)}, bf16[2,256,128]{2,1,0:T(8,128)(2,1)S(1)}, u32[]{:S(2)}, u32[]{:S(2)}) collective-permute-start(bf16[2,256,128]{2,1,0:T(8,128)(2,1)S(1)} %copy-done.5), channel_id=1, source_target_pairs={{0,4},{4,8},{8,12},{1,5},{5,9},{9,13},{2,6},{6,10},{10,14},{3,7},{... | collective-permute-start | bytes 393224 | tf_op jit(solution)/shard_map/ppermute | solution.py:37
  226.1 9.9 %copy-start.2 = (bf16[8,256,128]{2,1,0:T(8,128)(2,1)S(1)}, bf16[8,256,128]{2,1,0:T(8,128)(2,1)}, u32[]{:S(2)}) copy-start(bf16[8,256,128]{2,1,0:T(8,128)(2,1)} %param.16) | copy-start | bytes 1572868
  372.7 0.8 copy-start.6
  372.7 1.8 copy-start.1
